TPU v7x, 256 devices: a whole 4x4x8 slice. The times are simulated.
256 devices in a mesh: gz: 2 (over core), row: 4 (over x), col: 32 (over z, y).
Axes of the slice: x: 4, y: 4, z: 8, core: 2. Of those that a mesh axis runs over, the one named last changes fastest.
Arguments:
- front_matrix: float32 [4096, 4096], P('row', 'col'), may hold values from -6 to 6
- l_panels: float32 [2, 8, 4, 512, 256], P('gz', None, 'row', 'col'), may hold values from -6 to 6
- l_map: int32 [2, 8, 4, 512], P('gz', None, 'row'), may hold values from 0 to 1024, as said below
- u_panels: float32 [2, 8, 32, 64, 256], P('gz', None, 'col', 'row'), may hold values from -0.375 to 0.375
- u_map: int32 [2, 8, 32, 64], P('gz', None, 'col'), may hold values from 0 to 128, as said below
Outputs:
- updated_front: float32 [4096, 4096], P('row', 'col')
Inputs may be any that keep to these rules, and one draw needn't show every extreme that they name: l_map[z,h,p,:] lists distinct rows of row block p updated by child h of layer z, used slots first, listed block of 128 rows by block, at most 64 rows to a block; unused slots hold 1024; in every child some row block uses all 512 slots. u_map[z,h,q,:] lists distinct columns of column block q updated by child h of layer z, used slots first, listed block of 128 columns by block, at most 64 to a block; unused slots hold 128; in every child some column block uses all 64 slots.
All inputs are finite; a program needn't handle non-finite values.
Results may differ from a plain program's by a relative error of at most 0.0001.
Values sent between devices are 32-bit elements; how exact they have to be, the bound alone decides.
A program may use at most 64 MiB of HBM per device.

v0:
```python
import jax
import jax.numpy as jnp
from jax import lax
from jax.sharding import PartitionSpec as P


def spread_dense(row_panel, row_map, col_dense, row_count):
    targets = jnp.arange(row_count, dtype=jnp.int32)
    narrow = jnp.einsum("hik,hgk->hig", row_panel, col_dense, precision=lax.Precision.HIGHEST)
    row_hot = (row_map[:, :, None] == targets[None, None, :]).astype(jnp.float32)
    return jnp.einsum("hif,hig->fg", row_hot, narrow, precision=lax.Precision.HIGHEST)


def shards(front_matrix, l_panels, l_map, u_panels, u_map):
    row_count, col_count = front_matrix.shape
    row_map = l_map[0, :, 0, :]
    col_map = u_map[0, :, 0, :]
    col_panel = lax.all_gather(u_panels, "row", axis=3, tiled=True)[0, :, 0]
    col_targets = jnp.arange(col_count, dtype=jnp.int32)
    col_hot = (col_map[:, :, None] == col_targets[None, None, :]).astype(jnp.float32)
    col_dense = jnp.einsum("hjg,hjk->hgk", col_hot, col_panel, precision=lax.Precision.HIGHEST)
    row_panel = lax.all_gather(l_panels, "col", axis=3, tiled=True)[0, :, 0]
    update = spread_dense(row_panel, row_map, col_dense, row_count)
    summed = lax.psum(update, "gz")
    return front_matrix - summed


def solution(mesh):
    placed = (
        P("row", "col"),
        P("gz", None, "row", "col", None),
        P("gz", None, "row", None),
        P("gz", None, "col", "row", None),
        P("gz", None, "col", None),
    )
    return jax.shard_map(
        shards, mesh=mesh, in_specs=placed, out_specs=P("row", "col"), check_vma=False
    )
```

profile of v0, /device:TPU:1, one launch (start us, length us, event | category | flops | bytes accessed | tf_op | source)
XLA Modules:
  0.0 145.7 jit_solution(16361774498330991726)
XLA Ops:
  6.5 0.0 all-gather.2.cloned.1.call-start
  6.5 0.7 all-gather.2.cloned.1.call-update
  7.3 0.0 all-reduce.2.cloned.1.call-start
  7.3 0.7 copy.8
  8.0 12.5 %all_gather.6 = f32[1,8,1,64,256]{4,3,2,1,0:T(8,128)S(1)} all-gather(f32[1,8,1,16,256]{4,3,2,1,0:T(8,128)} %param.8), channel_id=1, replica_groups=mesh['gz'=2,'row'=4,'col'=32] {'row'}, dimensions={3}, use_global_device_ids=true | all-gather | bytes 655360 | tf_op jit(solution)/shard_map/all_gather | solution.py:18
  20.6 1.5 %fusion.8 = f32[8,128,256]{2,1,0:T(8,128)S(1)} fusion(f32[1,8,1,64,256]{4,3,2,1,0:T(8,128)S(1)} %all_gather.6, s32[8,64]{1,0:T(8,128)} %bitcast.19), kind=kOutput, calls=%fused_computation.7 | convolution fusion | flops 201392128 | bytes 1574912 | tf_op jit(solution)/shard_map/hjg,hjk->hgk/dot_general | solution.py:21
  22.1 70.8 %all-gather.2.cloned.1.call-done = f32[1,8,1,512,256]{4,3,2,1,0:T(8,128)} async-done(((f32[1,8,1,16,256]{4,3,2,1,0:T(8,128)}), f32[1,8,1,512,256]{4,3,2,1,0:T(8,128)}) %all-gather.2.cloned.1.call-update) | async-done | bytes 4194320 | tf_op jit(solution)/shard_map/all_gather | solution.py:22
  92.9 5.3 %fusion.2 = f32[8,128,512]{1,2,0:T(8,128)S(1)} fusion(f32[8,128,256]{2,1,0:T(8,128)S(1)} %fusion.8, f32[1,8,1,512,256]{4,3,2,1,0:T(8,128)} %all-gather.2.cloned.1.call-done), kind=kOutput, calls=%fused_computation.3 | convolution fusion | flops 1610612736 | bytes 7340032 | tf_op jit(solution)/shard_map/hik,hgk->hig/dot_general | solution.py:9
  98.3 0.0 copy-start
  98.3 8.4 %fusion.5 = f32[1024,128]{1,0:T(8,128)} fusion(f32[8,128,512]{1,2,0:T(8,128)S(1)} %fusion.2, s32[8,512]{1,0:T(8,128)S(1)} %bitcast.18), kind=kOutput, calls=%fused_computation.6 | convolution fusion | flops 6446645248 | bytes 2637824 | tf_op jit(solution)/shard_map/hif,hig->fg/dot_general | solution.py:11
  106.6 0.0 all-reduce.2.cloned.1.call-update
  106.7 30.3 %all-reduce.2.cloned.1.call-done = f32[1024,128]{1,0:T(8,128)} async-done(((f32[1024,128]{1,0:T(8,128)}), f32[1024,128]{1,0:T(8,128)}) %all-reduce.2.cloned.1.call-update) | async-done | bytes 524304 | tf_op jit(solution)/shard_map/psum | solution.py:24
  137.0 0.0 copy-done
  137.0 1.9 %sub.3 = f32[1024,128]{1,0:T(8,128)} subtract(f32[1024,128]{1,0:T(8,128)S(1)} %copy-done, f32[1024,128]{1,0:T(8,128)} %all-reduce.2.cloned.1.call-done) | non-fusion elementwise | flops 131072 | bytes 1572864 | tf_op jit(solution)/shard_map/sub | solution.py:25
Async XLA Ops:
  6.5 86.4 %all-gather.2.cloned.1.call-start = ((), (), s32[]{:S(2)}) async-start(), calls=%async_computation | async-start | bytes 4325376 | tf_op jit(solution)/shard_map/all_gather | solution.py:22
  7.3 129.7 %all-reduce.2.cloned.1.call-start = ((), (), s32[]{:S(2)}) async-start(), calls=%async_computation.1 | async-start | bytes 1048576 | tf_op jit(solution)/shard_map/psum | solution.py:24
  98.3 38.7 %copy-start = (f32[1024,128]{1,0:T(8,128)S(1)}, f32[1024,128]{1,0:T(8,128)}, u32[]{:S(2)}) copy-start(f32[1024,128]{1,0:T(8,128)} %param.5) | copy-start | bytes 1572868
Sparse Core Ops, SparseCore 0:
  9.9 82.9 all-gather.1
  106.8 30.1 all-reduce.1
where the time goes:
time: 146 us
  waiting for transfers between devices  102 us (70%)
  matrix products  15.3 us (10%)
  between operations  13.4 us (9%)
  blocking collectives  12.5 us (9%)
  other arithmetic  1.89 us (1%)
    all_gather x1, waiting for transfers between devices, shards(): row_panel = lax.all_gather(l_panels, 'col', axis=3, tiled=True)[0, :, 0]  70.8 us
    psum x1, waiting for transfers between devices, shards(): summed = lax.psum(update, 'gz')  30.3 us
    all_gather x1, blocking collectives, shards(): col_panel = lax.all_gather(u_panels, 'row', axis=3, tiled=True)[0, :, 0]  12.5 us
    dot_general x1, matrix products, spread_dense(): jnp.einsum('hif,hig->fg', row_hot, narrow, precision=lax.Precision.HIGHEST)  8.37 us
    dot_general x1, matrix products, spread_dense(): jnp.einsum('hik,hgk->hig', row_panel, col_dense, precision=lax.Precision....  5.34 us
  transfers between devices with their start and end apart: 2, of which 2 were waited for; matrix products, arithmetic and copies ran while one was open for 2% of the time, Pallas kernels for 0%

commit v1 on v0

v1 whole, which is shorter than its diff:
```python
import functools

import jax
import jax.numpy as jnp
from jax import lax
from jax.experimental import pallas as pl
from jax.experimental.pallas import tpu as pltpu
from jax.sharding import PartitionSpec as P

MESH = pl.DeviceIdType.MESH
F32 = jnp.float32
BF16 = jnp.bfloat16
NX, NY, NZ = 4, 4, 8
GROUPS = ((0, 1), (2, 7), (6, 3), (4, 5))
CHUNKS = 4


def split(value):
    high = value.astype(BF16)
    return high, (value - high.astype(F32)).astype(BF16)


def dot_nt(left, right):
    return lax.dot_general(left, right, (((1,), (1,)), ((), ())), preferred_element_type=F32)


def kernel(
    front, l_in, lmap, u_in, umap, out,
    lbuf, ubuf, whi, wlo, hot, col_hot, packed, recv, dense, acc, mine, other, front_v,
    uy_s, uy_r, ux_s, ux_r, ly_s, ly_r, zm_s, zp_s, z_r, res_s, res_r, ex_s, ex_r, loc,
):
    core, x, col = lax.axis_index("gz"), lax.axis_index("row"), lax.axis_index("col")
    y, z = lax.rem(col, NY), lax.div(col, NY)
    peer_y = [lax.rem(y + d, NY) for d in range(NY)]
    from_y = [lax.rem(y + NY - d, NY) for d in range(NY)]

    def at_y(d):
        return (core, x, z * NY + peer_y[d])

    def at_x(d):
        return (core, lax.rem(x + d, NX), col)

    def at_z(d):
        return (core, x, lax.rem(z + NZ + d, NZ) * NY + y)

    twin = (1 - core, x, col)
    peers = [at_y(d) for d in (1, 2, 3)] + [at_x(d) for d in (1, 2, 3)] + [at_z(1), at_z(-1), twin]
    barrier = pltpu.get_barrier_semaphore()
    for peer in peers:
        pl.semaphore_signal(barrier, inc=1, device_id=peer, device_id_type=MESH)
    fetch = pltpu.make_async_copy(front, front_v, loc.at[0])
    own_l = pltpu.make_async_copy(l_in.at[0, pl.ds(2 * y, 2), 0], lbuf.at[0, y], loc.at[1])
    own_u = pltpu.make_async_copy(u_in.at[0, pl.ds(2 * y, 2), 0], ubuf.at[x, y], loc.at[2])
    fetch.start()
    own_l.start()
    own_u.start()
    pl.semaphore_wait(barrier, len(peers))

    sent = []

    def send(src, dst, send_sem, recv_sem, device):
        copy = pltpu.make_async_remote_copy(
            src_ref=src, dst_ref=dst, send_sem=send_sem, recv_sem=recv_sem,
            device_id=device, device_id_type=MESH,
        )
        copy.start()
        sent.append(copy)
        return copy

    u_y, u_x, l_y = {}, {}, {}
    for d in (1, 3, 2):
        u_y[d] = send(
            u_in.at[0, pl.ds(2 * peer_y[d], 2), 0], ubuf.at[x, y], uy_s.at[d - 1], uy_r.at[d - 1], at_y(d)
        )
    for d in (1, 3, 2):
        u_x[d, 0] = send(
            u_in.at[0, pl.ds(2 * y, 2), 0], ubuf.at[x, y], ux_s.at[d - 1, 0], ux_r.at[d - 1, 0], at_x(d)
        )
    for d in (1, 3, 2):
        l_y[d] = send(
            l_in.at[0, pl.ds(2 * peer_y[d], 2), 0], lbuf.at[0, y], ly_s.at[d - 1], ly_r.at[d - 1], at_y(d)
        )

    zc = {}

    def z_send(rel, k, down, src=None):
        piece = from_y[k]
        src = lbuf.at[rel, piece] if src is None else src
        if down:
            to = rel + 1
            zc[to, k] = send(src, lbuf.at[to, piece], zm_s.at[rel, k], z_r.at[to, k], at_z(-1))
        else:
            to = (rel + NZ - 1) % NZ
            zc[to, k] = send(src, lbuf.at[to, piece], zp_s.at[rel, k], z_r.at[to, k], at_z(1))

    z_send(0, 0, True, l_in.at[0, pl.ds(2 * y, 2), 0])
    z_send(0, 0, False, l_in.at[0, pl.ds(2 * y, 2), 0])

    def z_pass(rel):
        for k in range(NY):
            zc[rel, k].wait_recv()
            if rel in (1, 2) or (rel == 3 and k < 2):
                z_send(rel, k, True)
            if rel in (7, 6) or (rel == 5 and k >= 2):
                z_send(rel, k, False)

    lane = lax.broadcasted_iota(jnp.int32, (1, 128), 1)

    col_ids = lax.broadcasted_iota(jnp.int32, (256, 128), 0)
    for h in range(8):
        single = umap[0, h]
        both = jnp.concatenate([single, single], axis=1)
        target = jnp.where(lane < 64, jnp.where(both < 128, both, -1), both + 128)
        col_hot[h] = (col_ids == target).astype(F32).astype(BF16)

    for d in (1, 3, 2):
        u_y[d].wait_recv()
        for dx in (1, 3, 2):
            piece = ubuf.at[x, from_y[d]]
            u_x[dx, d] = send(piece, piece, ux_s.at[dx - 1, d], ux_r.at[dx - 1, d], at_x(dx))
    for d in (1, 3, 2):
        l_y[d].wait_recv()
        z_send(0, d, True)
        z_send(0, d, False)

    shift = lax.rem(NZ - z, NZ) * 64

    def row_hots(tiles):
        for tile in tiles:
            d, c = divmod(tile, 2)
            turned = pltpu.roll(lmap[0, 2 * from_y[d] + c], shift, 1)
            t = [turned[:, 128 * i : 128 * i + 128] for i in range(4)]
            rows = (t[0], jnp.where(lane < 64, t[1], t[3]), jnp.where(lane < 64, t[3], t[1]), t[2])

            def fill(step, carry):
                base = pl.multiple_of(step * 64, 64)
                ids = lax.broadcasted_iota(jnp.int32, (64, 128), 0) + base
                for g in range(4):
                    hot[g, pl.ds(base, 64), tile * 128 : tile * 128 + 128] = (
                        (ids == rows[g]).astype(F32).astype(BF16)
                    )
                return carry

            lax.fori_loop(0, 16, fill, 0)

    row_hots((0, 1, 2, 3))
    z_pass(1)
    z_pass(7)
    row_hots((4, 5, 6, 7))

    own_u.wait()
    for k in range(NY):
        for dx in (1, 3, 2):
            u_x[dx, k].wait_recv()
    for c in range(2):
        for q in range(NY):
            high, low = split(ubuf[:, q, c].reshape(64, 256))
            whi[c, 64 * q : 64 * q + 64] = high
            wlo[c, 64 * q : 64 * q + 64] = low
    own_l.wait()

    rc = {}

    def multiply(g):
        first, second = GROUPS[g]
        for c in range(2):
            left = jnp.concatenate(
                [lbuf[first, :, c].reshape(64, 256), lbuf[second, :, c].reshape(64, 256)], axis=0
            )
            high, low = split(left)
            prod = dot_nt(high, wlo[c]) + dot_nt(low, whi[c]) + dot_nt(high, whi[c])
            for j in range(2):
                top = prod[:64, 128 * j : 128 * j + 128]
                bottom = prod[64:, 128 * j : 128 * j + 128]
                packed[g, c, 2 * j] = jnp.where(lane < 64, top, pltpu.roll(bottom, 64, 1))
                packed[g, c, 2 * j + 1] = jnp.where(lane < 64, pltpu.roll(top, 64, 1), bottom)
            for d in (2, 1, 3):
                rc[g, c, d] = send(
                    packed.at[g, c, peer_y[d]], recv.at[g, c, d - 1],
                    res_s.at[g, c, d - 1], res_r.at[g, c, d - 1], at_y(d),
                )

    def expand(g):
        for d in (0, 1, 3, 2):
            for c in range(2):
                if d == 0:
                    value = packed[g, c, y]
                else:
                    rc[g, c, d].wait_recv()
                    value = recv[g, c, d - 1]
                high, low = split(value)
                wide = dot_nt(jnp.concatenate([high, low], axis=0), col_hot[2 * from_y[d] + c]).astype(BF16)
                at = (2 * d + c) * 128
                dense[at : at + 64, :128] = wide[:64, :128]
                dense[at + 64 : at + 128, :128] = wide[:64, 128:]
                dense[at : at + 64, 128:] = wide[64:, :128]
                dense[at + 64 : at + 128, 128:] = wide[64:, 128:]

    size = 1024 // CHUNKS

    def scatter(g, chunk):
        rows = slice(chunk * size, chunk * size + size)
        both = jnp.dot(hot[g, rows], dense[...], preferred_element_type=F32)
        return both[:, :128] + both[:, 128:]

    multiply(0)
    z_pass(2)
    z_pass(6)
    multiply(1)
    z_pass(3)
    z_pass(5)
    multiply(2)
    z_pass(4)
    multiply(3)

    for g in range(3):
        expand(g)
        for chunk in range(CHUNKS):
            rows = slice(chunk * size, chunk * size + size)
            part = scatter(g, chunk)
            acc[rows] = part if g == 0 else acc[rows] + part
    expand(3)
    ex = []
    for chunk in range(CHUNKS):
        rows = slice(chunk * size, chunk * size + size)
        mine[rows] = acc[rows] + scatter(3, chunk)
        ex.append(send(mine.at[rows], other.at[rows], ex_s.at[chunk], ex_r.at[chunk], twin))
    fetch.wait()
    for chunk in range(CHUNKS):
        rows = slice(chunk * size, chunk * size + size)
        ex[chunk].wait_recv()
        out[rows] = front_v[rows] - (mine[rows] + other[rows])
    for copy in sent:
        copy.wait_send()


def shards(front_matrix, l_panels, l_map, u_panels, u_map):
    hbm = pl.BlockSpec(memory_space=pltpu.HBM)
    vmem = pl.BlockSpec(memory_space=pltpu.VMEM)
    dma = pltpu.SemaphoreType.DMA
    return pl.pallas_call(
        kernel,
        out_shape=jax.ShapeDtypeStruct((1024, 128), F32),
        in_specs=[hbm, hbm, vmem, hbm, vmem],
        out_specs=vmem,
        scratch_shapes=[
            pltpu.VMEM((NZ, NY, 2, 16, 256), F32),
            pltpu.VMEM((NX, NY, 2, 16, 256), F32),
            pltpu.VMEM((2, 256, 256), BF16),
            pltpu.VMEM((2, 256, 256), BF16),
            pltpu.VMEM((4, 1024, 1024), BF16),
            pltpu.VMEM((8, 256, 128), BF16),
            pltpu.VMEM((4, 2, NY, 64, 128), F32),
            pltpu.VMEM((4, 2, 3, 64, 128), F32),
            pltpu.VMEM((1024, 256), BF16),
            pltpu.VMEM((1024, 128), F32),
            pltpu.VMEM((1024, 128), F32),
            pltpu.VMEM((1024, 128), F32),
            pltpu.VMEM((1024, 128), F32),
            dma((3,)), dma((3,)), dma((3, 4)), dma((3, 4)), dma((3,)), dma((3,)),
            dma((NZ, 4)), dma((NZ, 4)), dma((NZ, 4)),
            dma((4, 2, 3)), dma((4, 2, 3)), dma((CHUNKS,)), dma((CHUNKS,)), dma((3,)),
        ],
        compiler_params=pltpu.CompilerParams(
            collective_id=0, has_side_effects=True, vmem_limit_bytes=48 << 20
        ),
        name="extend_add",
    )(front_matrix, l_panels, l_map, u_panels, u_map)


def solution(mesh):
    placed = (
        P("row", "col"),
        P("gz", None, "row", "col", None),
        P("gz", None, "row", None),
        P("gz", None, "col", "row", None),
        P("gz", None, "col", None),
    )
    return jax.shard_map(
        shards, mesh=mesh, in_specs=placed, out_specs=P("row", "col"), check_vma=False
    )
```

time: 146 us -> 47.7 us (0.33)
  waiting for transfers between devices: 102 us -> 0 us
  Pallas kernels: 0 us -> 42.4 us
  matrix products: 15.3 us -> 0 us
  between operations: 13.4 us -> 0.01 us
  blocking collectives: 12.5 us -> 0 us
  local copies, waits for them, and re-layouts: 0.73 us -> 5.05 us
  other arithmetic: 1.89 us -> 0 us
    all_gather x1 -> x0, waiting for transfers between devices: 70.8 us -> none  [shards(): row_panel = lax.all_gather(l_panels, 'col', axis=3, tiled=True)[0, :, 0]]
    pallas_call x0 -> x1, Pallas kernels: none -> 42.4 us  [shards(): pl.pallas_call(kernel, out_shape=jax.ShapeDtypeStruct((1024, 128), F32),...]
    psum x1 -> x0, waiting for transfers between devices: 30.3 us -> none  [shards(): summed = lax.psum(update, 'gz')]
    dot_general x3 -> x0, matrix products: 15.3 us -> none  [the longest x1 8.37 us: spread_dense(): jnp.einsum('hif,hig->fg', row_hot, narrow, precision=lax.Precision.HIGHEST)]
    all_gather x1 -> x0, blocking collectives: 12.5 us -> none  [shards(): col_panel = lax.all_gather(u_panels, 'row', axis=3, tiled=True)[0, :, 0]]
    unnamed x3 -> x11, local copies, waits for them, and re-layouts: 0.73 us -> 5.05 us
    sub x1 -> x0, other arithmetic: 1.89 us -> none  [shards(): return front_matrix - summed]
  transfers between devices with their start and end apart: 2 -> 0, of which waited for: 2 -> 0; matrix products, arithmetic and copies ran while one was open for 2% -> 0% of each run, Pallas kernels for 0% -> 0%
where the time goes in v1:
time: 47.7 us; the launch traced here: 47.4 us
  Pallas kernels  42.4 us (89%)
  local copies, waits for them, and re-layouts  5.05 us (11%)
    pallas_call x1, Pallas kernels, shards(): pl.pallas_call(kernel, out_shape=jax.ShapeDtypeStruct((1024, 128), F32),...  42.4 us
    unnamed x11, local copies, waits for them, and re-layouts  5.05 us

profile of v1, /device:TPU:1, one launch (start us, length us, event | category | flops | bytes accessed | tf_op | source)
XLA Modules:
  0.0 47.4 jit_solution(14771866168478079339)
XLA Ops:
  0.0 0.0 copy-start
  0.0 1.0 %copy-done = f32[1024,128]{1,0:T(8,128)S(1)} copy-done((f32[1024,128]{1,0:T(8,128)S(1)}, f32[1024,128]{1,0:T(8,128)}, u32[]{:S(2)}) %copy-start) | copy-done | bytes 524312
  1.0 0.0 copy-start.1
  1.0 0.9 %copy-done.1 = f32[1,8,1,16,256]{4,3,2,1,0:T(8,128)S(1)} copy-done((f32[1,8,1,16,256]{4,3,2,1,0:T(8,128)S(1)}, f32[1,8,1,16,256]{4,3,2,1,0:T(8,128)}, u32[]{:S(2)}) %copy-start.1) | copy-done | bytes 131096
  1.9 0.0 copy-start.2
  1.9 0.9 %copy-done.2 = f32[1,8,1,16,256]{4,3,2,1,0:T(8,128)S(1)} copy-done((f32[1,8,1,16,256]{4,3,2,1,0:T(8,128)S(1)}, f32[1,8,1,16,256]{4,3,2,1,0:T(8,128)}, u32[]{:S(2)}) %copy-start.2) | copy-done | bytes 131096
  2.9 0.0 copy-start.3
  2.9 0.7 %copy-done.3 = s32[1,8,1,512]{3,2,1,0:T(1,128)S(1)} copy-done((s32[1,8,1,512]{3,2,1,0:T(1,128)S(1)}, s32[1,8,1,512]{3,2,1,0:T(1,128)}, u32[]{:S(2)}) %copy-start.3) | copy-done | bytes 16408
  3.6 0.0 copy-start.4
  3.6 0.7 %copy-done.4 = s32[1,8,1,64]{3,2,1,0:T(1,128)S(1)} copy-done((s32[1,8,1,64]{3,2,1,0:T(1,128)S(1)}, s32[1,8,1,64]{3,2,1,0:T(1,128)}, u32[]{:S(2)}) %copy-start.4) | copy-done | bytes 2072
  4.3 42.4 %extend_add.1 = f32[1024,128]{1,0:T(8,128)S(1)} custom-call(f32[1024,128]{1,0:T(8,128)S(1)} %copy-done, f32[1,8,1,16,256]{4,3,2,1,0:T(8,128)S(1)} %copy-done.1, s32[1,8,1,512]{3,2,1,0:T(1,128)S(1)} %copy-done.3, f32[1,8,1,16,256]{4,3,2,1,0:T(8,128)S(1)} %copy-done.2, s32[1,8,1,64]{3,2,1,0:T(1,128)S(1)} %copy-done.4), custom_call_target="tpu_custom_call" | custom-call | tf_op jit(solution)/shard_map/extend_add/pallas_call | solution.py:241
  46.6 0.8 %copy.7 = f32[1024,128]{1,0:T(8,128)} copy(f32[1024,128]{1,0:T(8,128)S(1)} %extend_add.1) | data formatting | bytes 1048576
Async XLA Ops:
  0.0 1.0 %copy-start = (f32[1024,128]{1,0:T(8,128)S(1)}, f32[1024,128]{1,0:T(8,128)}, u32[]{:S(2)}) copy-start(f32[1024,128]{1,0:T(8,128)} %front.1) | copy-start | bytes 1572868
  1.0 0.9 %copy-start.1 = (f32[1,8,1,16,256]{4,3,2,1,0:T(8,128)S(1)}, f32[1,8,1,16,256]{4,3,2,1,0:T(8,128)}, u32[]{:S(2)}) copy-start(f32[1,8,1,16,256]{4,3,2,1,0:T(8,128)} %l_in.1) | copy-start | bytes 393220
  1.9 0.9 %copy-start.2 = (f32[1,8,1,16,256]{4,3,2,1,0:T(8,128)S(1)}, f32[1,8,1,16,256]{4,3,2,1,0:T(8,128)}, u32[]{:S(2)}) copy-start(f32[1,8,1,16,256]{4,3,2,1,0:T(8,128)} %u_in.1) | copy-start | bytes 393220
  2.9 0.7 %copy-start.3 = (s32[1,8,1,512]{3,2,1,0:T(1,128)S(1)}, s32[1,8,1,512]{3,2,1,0:T(1,128)}, u32[]{:S(2)}) copy-start(s32[1,8,1,512]{3,2,1,0:T(1,128)} %lmap.1) | copy-start | bytes 49156
  3.6 0.7 %copy-start.4 = (s32[1,8,1,64]{3,2,1,0:T(1,128)S(1)}, s32[1,8,1,64]{3,2,1,0:T(1,128)}, u32[]{:S(2)}) copy-start(s32[1,8,1,64]{3,2,1,0:T(1,128)} %umap.1) | copy-start | bytes 6148

commit v2 on v1

--- a/solution.py
+++ b/solution.py
@@ -25,9 +25,9 @@
 
 
 def kernel(
-    front, l_in, lmap, u_in, umap, out,
-    lbuf, ubuf, whi, wlo, hot, col_hot, packed, recv, dense, acc, mine, other, front_v,
-    uy_s, uy_r, ux_s, ux_r, ly_s, ly_r, zm_s, zp_s, z_r, res_s, res_r, ex_s, ex_r, loc,
+    front, l_in, lmap_in, u_in, umap_in, out,
+    lbuf, ubuf, whi, wlo, hot, col_hot, packed, recv, dense, acc, mine, other, front_v, lmap, umap,
+    uy_s, uy_r, ux_s, ux_r, ly_s, zm_s, zp_s, z_r, res_s, res_r, ex_s, ex_r, loc,
 ):
     core, x, col = lax.axis_index("gz"), lax.axis_index("row"), lax.axis_index("col")
     y, z = lax.rem(col, NY), lax.div(col, NY)
@@ -40,17 +40,24 @@
     def at_x(d):
         return (core, lax.rem(x + d, NX), col)
 
-    def at_z(d):
-        return (core, x, lax.rem(z + NZ + d, NZ) * NY + y)
+    def at_z(d, dy=0):
+        return (core, x, lax.rem(z + NZ + d, NZ) * NY + peer_y[dy])
 
     twin = (1 - core, x, col)
-    peers = [at_y(d) for d in (1, 2, 3)] + [at_x(d) for d in (1, 2, 3)] + [at_z(1), at_z(-1), twin]
+    peers = [at_y(d) for d in (1, 2, 3)] + [at_x(d) for d in (1, 2, 3)] + [twin]
+    peers += [at_z(d, dy) for d in (1, -1) for dy in range(NY)]
     barrier = pltpu.get_barrier_semaphore()
     for peer in peers:
         pl.semaphore_signal(barrier, inc=1, device_id=peer, device_id_type=MESH)
     fetch = pltpu.make_async_copy(front, front_v, loc.at[0])
     own_l = pltpu.make_async_copy(l_in.at[0, pl.ds(2 * y, 2), 0], lbuf.at[0, y], loc.at[1])
-    own_u = pltpu.make_async_copy(u_in.at[0, pl.ds(2 * y, 2), 0], ubuf.at[x, y], loc.at[2])
+    maps = (
+        pltpu.make_async_copy(lmap_in.at[0], lmap, loc.at[3]),
+        pltpu.make_async_copy(umap_in.at[0], umap, loc.at[4]),
+    )
+    own_u = pltpu.make_async_copy(u_in.at[0, pl.ds(2 * y, 2), 0], ubuf.at[:, x, y], loc.at[2])
+    for copy in maps:
+        copy.start()
     fetch.start()
     own_l.start()
     own_u.start()
@@ -67,19 +74,30 @@
         sent.append(copy)
         return copy
 
-    u_y, u_x, l_y = {}, {}, {}
-    for d in (1, 3, 2):
-        u_y[d] = send(
-            u_in.at[0, pl.ds(2 * peer_y[d], 2), 0], ubuf.at[x, y], uy_s.at[d - 1], uy_r.at[d - 1], at_y(d)
-        )
-    for d in (1, 3, 2):
-        u_x[d, 0] = send(
-            u_in.at[0, pl.ds(2 * y, 2), 0], ubuf.at[x, y], ux_s.at[d - 1, 0], ux_r.at[d - 1, 0], at_x(d)
-        )
-    for d in (1, 3, 2):
-        l_y[d] = send(
-            l_in.at[0, pl.ds(2 * peer_y[d], 2), 0], lbuf.at[0, y], ly_s.at[d - 1], ly_r.at[d - 1], at_y(d)
-        )
+    u_y, u_x = {}, {}
+
+    def u_spread(c):
+        for d in (1, 3, 2):
+            u_y[d, c] = send(
+                u_in.at[0, 2 * peer_y[d] + c, 0], ubuf.at[c, x, y],
+                uy_s.at[d - 1, c], uy_r.at[d - 1, c], at_y(d),
+            )
+
+    def u_own(c):
+        for d in (1, 3, 2):
+            u_x[d, 0, c] = send(
+                u_in.at[0, 2 * y + c, 0], ubuf.at[c, x, y],
+                ux_s.at[d - 1, 0, c], ux_r.at[d - 1, 0, c], at_x(d),
+            )
+
+    def u_pass(c):
+        for k in (1, 3, 2):
+            u_y[k, c].wait_recv()
+            piece = ubuf.at[c, x, from_y[k]]
+            for d in (1, 3, 2):
+                u_x[d, k, c] = send(
+                    piece, piece, ux_s.at[d - 1, k, c], ux_r.at[d - 1, k, c], at_x(d)
+                )
 
     zc = {}
 
@@ -93,42 +111,29 @@
             to = (rel + NZ - 1) % NZ
             zc[to, k] = send(src, lbuf.at[to, piece], zp_s.at[rel, k], z_r.at[to, k], at_z(1))
 
-    z_send(0, 0, True, l_in.at[0, pl.ds(2 * y, 2), 0])
-    z_send(0, 0, False, l_in.at[0, pl.ds(2 * y, 2), 0])
-
-    def z_pass(rel):
-        for k in range(NY):
-            zc[rel, k].wait_recv()
-            if rel in (1, 2) or (rel == 3 and k < 2):
-                z_send(rel, k, True)
-            if rel in (7, 6) or (rel == 5 and k >= 2):
-                z_send(rel, k, False)
+    def z_pass(step, pieces=(1, 3, 2)):
+        for k in pieces:
+            for rel, down in ((step, True), (NZ - step, False)):
+                zc[rel, k].wait_recv()
+                if step < 3 or down == (k in (0, 2)):
+                    z_send(rel, k, down)
 
     lane = lax.broadcasted_iota(jnp.int32, (1, 128), 1)
 
-    col_ids = lax.broadcasted_iota(jnp.int32, (256, 128), 0)
-    for h in range(8):
-        single = umap[0, h]
-        both = jnp.concatenate([single, single], axis=1)
-        target = jnp.where(lane < 64, jnp.where(both < 128, both, -1), both + 128)
-        col_hot[h] = (col_ids == target).astype(F32).astype(BF16)
-
-    for d in (1, 3, 2):
-        u_y[d].wait_recv()
-        for dx in (1, 3, 2):
-            piece = ubuf.at[x, from_y[d]]
-            u_x[dx, d] = send(piece, piece, ux_s.at[dx - 1, d], ux_r.at[dx - 1, d], at_x(dx))
-    for d in (1, 3, 2):
-        l_y[d].wait_recv()
-        z_send(0, d, True)
-        z_send(0, d, False)
+    def column_hots():
+        col_ids = lax.broadcasted_iota(jnp.int32, (256, 128), 0)
+        for h in range(8):
+            single = umap[h]
+            both = jnp.concatenate([single, single], axis=1)
+            target = jnp.where(lane < 64, jnp.where(both < 128, both, -1), both + 128)
+            col_hot[h] = (col_ids == target).astype(F32).astype(BF16)
 
     shift = lax.rem(NZ - z, NZ) * 64
 
     def row_hots(tiles):
         for tile in tiles:
             d, c = divmod(tile, 2)
-            turned = pltpu.roll(lmap[0, 2 * from_y[d] + c], shift, 1)
+            turned = pltpu.roll(lmap[2 * from_y[d] + c], shift, 1)
             t = [turned[:, 128 * i : 128 * i + 128] for i in range(4)]
             rows = (t[0], jnp.where(lane < 64, t[1], t[3]), jnp.where(lane < 64, t[3], t[1]), t[2])
 
@@ -143,27 +148,20 @@
 
             lax.fori_loop(0, 16, fill, 0)
 
-    row_hots((0, 1, 2, 3))
-    z_pass(1)
-    z_pass(7)
-    row_hots((4, 5, 6, 7))
-
-    own_u.wait()
-    for k in range(NY):
-        for dx in (1, 3, 2):
-            u_x[dx, k].wait_recv()
-    for c in range(2):
+    def u_join(c):
+        for k in (0, 1, 3, 2):
+            for d in (1, 3, 2):
+                u_x[d, k, c].wait_recv()
         for q in range(NY):
-            high, low = split(ubuf[:, q, c].reshape(64, 256))
+            high, low = split(ubuf[c, :, q].reshape(64, 256))
             whi[c, 64 * q : 64 * q + 64] = high
             wlo[c, 64 * q : 64 * q + 64] = low
-    own_l.wait()
 
     rc = {}
 
-    def multiply(g):
+    def multiply(g, children=(0, 1)):
         first, second = GROUPS[g]
-        for c in range(2):
+        for c in children:
             left = jnp.concatenate(
                 [lbuf[first, :, c].reshape(64, 256), lbuf[second, :, c].reshape(64, 256)], axis=0
             )
@@ -203,22 +201,58 @@
         both = jnp.dot(hot[g, rows], dense[...], preferred_element_type=F32)
         return both[:, :128] + both[:, 128:]
 
-    multiply(0)
-    z_pass(2)
-    z_pass(6)
-    multiply(1)
-    z_pass(3)
-    z_pass(5)
-    multiply(2)
-    z_pass(4)
-    multiply(3)
-
-    for g in range(3):
+    def update(g):
         expand(g)
         for chunk in range(CHUNKS):
             rows = slice(chunk * size, chunk * size + size)
             part = scatter(g, chunk)
             acc[rows] = part if g == 0 else acc[rows] + part
+
+    for down in (True, False):
+        z_send(0, 0, down, l_in.at[0, pl.ds(2 * y, 2), 0])
+    u_spread(0)
+    u_own(0)
+    for d in (1, 3, 2):
+        src = l_in.at[0, pl.ds(2 * peer_y[d], 2), 0]
+        zc[1, d] = send(src, lbuf.at[1, y], ly_s.at[d - 1, 1], z_r.at[1, d], at_z(-1, d))
+        zc[7, d] = send(src, lbuf.at[7, y], ly_s.at[d - 1, 2], z_r.at[7, d], at_z(1, d))
+    u_spread(1)
+    u_own(1)
+    for d in (1, 3, 2):
+        src = l_in.at[0, pl.ds(2 * peer_y[d], 2), 0]
+        zc[0, d] = send(src, lbuf.at[0, y], ly_s.at[d - 1, 0], z_r.at[0, d], at_y(d))
+    for copy in maps:
+        copy.wait()
+    row_hots((0,))
+    z_pass(1, (0,))
+    u_pass(0)
+    z_pass(1)
+    u_pass(1)
+    z_pass(2, (0,))
+    row_hots((1, 2))
+    z_pass(2, (1,))
+    z_pass(3, (0,))
+    own_u.wait()
+    own_l.wait()
+    for d in (1, 3, 2):
+        zc[0, d].wait_recv()
+    u_join(0)
+    multiply(0, (0,))
+    z_pass(2, (3, 2))
+    u_join(1)
+    multiply(0, (1,))
+    z_pass(3, (1,))
+    multiply(1)
+    z_pass(3, (3, 2))
+    multiply(2)
+    row_hots((3, 4, 5, 6, 7))
+    column_hots()
+    update(0)
+    for k in (0, 1, 3, 2):
+        zc[4, k].wait_recv()
+    multiply(3)
+    update(1)
+    update(2)
     expand(3)
     ex = []
     for chunk in range(CHUNKS):
@@ -236,16 +270,20 @@
 
 def shards(front_matrix, l_panels, l_map, u_panels, u_map):
     hbm = pl.BlockSpec(memory_space=pltpu.HBM)
+    operands = [
+        pltpu.with_memory_space_constraint(operand, pltpu.HBM)
+        for operand in (front_matrix, l_panels, l_map, u_panels, u_map)
+    ]
     vmem = pl.BlockSpec(memory_space=pltpu.VMEM)
     dma = pltpu.SemaphoreType.DMA
     return pl.pallas_call(
         kernel,
         out_shape=jax.ShapeDtypeStruct((1024, 128), F32),
-        in_specs=[hbm, hbm, vmem, hbm, vmem],
+        in_specs=[hbm] * 5,
         out_specs=vmem,
         scratch_shapes=[
             pltpu.VMEM((NZ, NY, 2, 16, 256), F32),
-            pltpu.VMEM((NX, NY, 2, 16, 256), F32),
+            pltpu.VMEM((2, NX, NY, 16, 256), F32),
             pltpu.VMEM((2, 256, 256), BF16),
             pltpu.VMEM((2, 256, 256), BF16),
             pltpu.VMEM((4, 1024, 1024), BF16),
@@ -257,15 +295,17 @@
             pltpu.VMEM((1024, 128), F32),
             pltpu.VMEM((1024, 128), F32),
             pltpu.VMEM((1024, 128), F32),
-            dma((3,)), dma((3,)), dma((3, 4)), dma((3, 4)), dma((3,)), dma((3,)),
+            pltpu.VMEM((8, 1, 512), jnp.int32),
+            pltpu.VMEM((8, 1, 64), jnp.int32),
+            dma((3, 2)), dma((3, 2)), dma((3, 4, 2)), dma((3, 4, 2)), dma((3, 3)),
             dma((NZ, 4)), dma((NZ, 4)), dma((NZ, 4)),
-            dma((4, 2, 3)), dma((4, 2, 3)), dma((CHUNKS,)), dma((CHUNKS,)), dma((3,)),
+            dma((4, 2, 3)), dma((4, 2, 3)), dma((CHUNKS,)), dma((CHUNKS,)), dma((5,)),
         ],
         compiler_params=pltpu.CompilerParams(
             collective_id=0, has_side_effects=True, vmem_limit_bytes=48 << 20
         ),
         name="extend_add",
-    )(front_matrix, l_panels, l_map, u_panels, u_map)
+    )(*operands)
 
 
 def solution(mesh):

time: 47.7 us -> 42.5 us (0.89)
  local copies, waits for them, and re-layouts: 5.05 us -> 0.8 us
  Pallas kernels: 42.4 us -> 41.6 us
    unnamed x11 -> x1, local copies, waits for them, and re-layouts: 5.05 us -> 0.8 us
    pallas_call x1, Pallas kernels: 42.4 us -> 41.6 us  [shards(): pl.pallas_call(kernel, out_shape=jax.ShapeDtypeStruct((1024, 128), F32),...]
where the time goes in v2:
time: 42.5 us; the launch traced here: 42.4 us
  Pallas kernels  41.6 us (98%)
  local copies, waits for them, and re-layouts  0.8 us (2%)
    pallas_call x1, Pallas kernels, shards(): pl.pallas_call(kernel, out_shape=jax.ShapeDtypeStruct((1024, 128), F32),...  41.6 us

profile of v2, /device:TPU:1, one launch (start us, length us, event | category | flops | bytes accessed | tf_op | source)
XLA Modules:
  0.0 42.4 jit_solution(991972107170662611)
XLA Ops:
  0.0 41.6 %extend_add.1 = f32[1024,128]{1,0:T(8,128)S(1)} custom-call(f32[1024,128]{1,0:T(8,128)} %front.1, f32[1,8,1,16,256]{4,3,2,1,0:T(8,128)} %l_in.1, s32[1,8,1,512]{3,2,1,0:T(1,128)} %lmap_in.1, f32[1,8,1,16,256]{4,3,2,1,0:T(8,128)} %u_in.1, s32[1,8,1,64]{3,2,1,0:T(1,128)} %umap_in.1), custom_call_target="tpu_custom_call" | custom-call | tf_op jit(solution)/shard_map/extend_add/pallas_call | solution.py:279
  41.6 0.8 %copy.7 = f32[1024,128]{1,0:T(8,128)} copy(f32[1024,128]{1,0:T(8,128)S(1)} %extend_add.1) | data formatting | bytes 1048576

commit v3 on v2

--- a/solution.py
+++ b/solution.py
@@ -27,7 +27,7 @@
 def kernel(
     front, l_in, lmap_in, u_in, umap_in, out,
     lbuf, ubuf, whi, wlo, hot, col_hot, packed, recv, dense, acc, mine, other, front_v, lmap, umap,
-    uy_s, uy_r, ux_s, ux_r, ly_s, zm_s, zp_s, z_r, res_s, res_r, ex_s, ex_r, loc,
+    uy_s, uy_r, ux_s, ux_r, ly_s, z_s, z_r, res_s, res_r, ex_s, ex_r, loc,
 ):
     core, x, col = lax.axis_index("gz"), lax.axis_index("row"), lax.axis_index("col")
     y, z = lax.rem(col, NY), lax.div(col, NY)
@@ -45,7 +45,7 @@
 
     twin = (1 - core, x, col)
     peers = [at_y(d) for d in (1, 2, 3)] + [at_x(d) for d in (1, 2, 3)] + [twin]
-    peers += [at_z(d, dy) for d in (1, -1) for dy in range(NY)]
+    peers += [at_z(d, dy) for d in (1, -1, 2, -2) for dy in range(NY)]
     barrier = pltpu.get_barrier_semaphore()
     for peer in peers:
         pl.semaphore_signal(barrier, inc=1, device_id=peer, device_id_type=MESH)
@@ -101,22 +101,24 @@
 
     zc = {}
 
-    def z_send(rel, k, down, src=None):
-        piece = from_y[k]
-        src = lbuf.at[rel, piece] if src is None else src
-        if down:
-            to = rel + 1
-            zc[to, k] = send(src, lbuf.at[to, piece], zm_s.at[rel, k], z_r.at[to, k], at_z(-1))
-        else:
-            to = (rel + NZ - 1) % NZ
-            zc[to, k] = send(src, lbuf.at[to, piece], zp_s.at[rel, k], z_r.at[to, k], at_z(1))
+    def z_start(reach, distances):
+        for d in distances:
+            src = l_in.at[0, pl.ds(2 * peer_y[d], 2), 0]
+            for dz in (-reach, reach):
+                rel = (-dz) % NZ
+                zc[rel, d] = send(src, lbuf.at[rel, y], z_s.at[rel, d], z_r.at[rel, d], at_z(dz, d))
 
     def z_pass(step, pieces=(1, 3, 2)):
         for k in pieces:
-            for rel, down in ((step, True), (NZ - step, False)):
+            for rel, dz in ((step, -1), (NZ - step, 1)):
                 zc[rel, k].wait_recv()
-                if step < 3 or down == (k in (0, 2)):
-                    z_send(rel, k, down)
+                if step == 2 or (step == 3 and (dz < 0) == (k in (0, 2))):
+                    to = rel - dz
+                    slot = to if to != 4 else (4 if dz < 0 else 0)
+                    zc[to, k] = send(
+                        lbuf.at[rel, from_y[k]], lbuf.at[to, from_y[k]],
+                        z_s.at[slot, k], z_r.at[to, k], at_z(dz),
+                    )
 
     lane = lax.broadcasted_iota(jnp.int32, (1, 128), 1)
 
@@ -172,7 +174,7 @@
                 bottom = prod[64:, 128 * j : 128 * j + 128]
                 packed[g, c, 2 * j] = jnp.where(lane < 64, top, pltpu.roll(bottom, 64, 1))
                 packed[g, c, 2 * j + 1] = jnp.where(lane < 64, pltpu.roll(top, 64, 1), bottom)
-            for d in (2, 1, 3):
+            for d in (1, 3, 2):
                 rc[g, c, d] = send(
                     packed.at[g, c, peer_y[d]], recv.at[g, c, d - 1],
                     res_s.at[g, c, d - 1], res_r.at[g, c, d - 1], at_y(d),
@@ -208,40 +210,35 @@
             part = scatter(g, chunk)
             acc[rows] = part if g == 0 else acc[rows] + part
 
-    for down in (True, False):
-        z_send(0, 0, down, l_in.at[0, pl.ds(2 * y, 2), 0])
+    z_start(1, (0,))
+    z_start(2, (0,))
     u_spread(0)
     u_own(0)
+    z_start(2, (1, 3, 2))
+    u_spread(1)
+    u_own(1)
+    z_start(1, (1, 3, 2))
     for d in (1, 3, 2):
         src = l_in.at[0, pl.ds(2 * peer_y[d], 2), 0]
-        zc[1, d] = send(src, lbuf.at[1, y], ly_s.at[d - 1, 1], z_r.at[1, d], at_z(-1, d))
-        zc[7, d] = send(src, lbuf.at[7, y], ly_s.at[d - 1, 2], z_r.at[7, d], at_z(1, d))
-    u_spread(1)
-    u_own(1)
-    for d in (1, 3, 2):
-        src = l_in.at[0, pl.ds(2 * peer_y[d], 2), 0]
-        zc[0, d] = send(src, lbuf.at[0, y], ly_s.at[d - 1, 0], z_r.at[0, d], at_y(d))
+        zc[0, d] = send(src, lbuf.at[0, y], ly_s.at[d - 1], z_r.at[0, d], at_y(d))
     for copy in maps:
         copy.wait()
-    row_hots((0,))
-    z_pass(1, (0,))
+    row_hots((0, 1, 2))
+    z_pass(2, (0,))
     u_pass(0)
-    z_pass(1)
     u_pass(1)
-    z_pass(2, (0,))
-    row_hots((1, 2))
-    z_pass(2, (1,))
+    z_pass(2)
     z_pass(3, (0,))
     own_u.wait()
     own_l.wait()
     for d in (1, 3, 2):
         zc[0, d].wait_recv()
+    z_pass(1, (0, 1, 3, 2))
     u_join(0)
     multiply(0, (0,))
-    z_pass(2, (3, 2))
+    z_pass(3, (1,))
     u_join(1)
     multiply(0, (1,))
-    z_pass(3, (1,))
     multiply(1)
     z_pass(3, (3, 2))
     multiply(2)
@@ -297,8 +294,8 @@
             pltpu.VMEM((1024, 128), F32),
             pltpu.VMEM((8, 1, 512), jnp.int32),
             pltpu.VMEM((8, 1, 64), jnp.int32),
-            dma((3, 2)), dma((3, 2)), dma((3, 4, 2)), dma((3, 4, 2)), dma((3, 3)),
-            dma((NZ, 4)), dma((NZ, 4)), dma((NZ, 4)),
+            dma((3, 2)), dma((3, 2)), dma((3, 4, 2)), dma((3, 4, 2)), dma((3,)),
+            dma((NZ, 4)), dma((NZ, 4)),
             dma((4, 2, 3)), dma((4, 2, 3)), dma((CHUNKS,)), dma((CHUNKS,)), dma((5,)),
         ],
         compiler_params=pltpu.CompilerParams(

time: 42.5 us -> 41.6 us (0.979)
  Pallas kernels: 41.6 us -> 40.7 us
    pallas_call x1, Pallas kernels: 41.6 us -> 40.7 us  [shards(): pl.pallas_call(kernel, out_shape=jax.ShapeDtypeStruct((1024, 128), F32),...]
where the time goes in v3:
time: 41.6 us; the launch traced here: 41.5 us
  Pallas kernels  40.7 us (98%)
  local copies, waits for them, and re-layouts  0.8 us (2%)
    pallas_call x1, Pallas kernels, shards(): pl.pallas_call(kernel, out_shape=jax.ShapeDtypeStruct((1024, 128), F32),...  40.7 us

profile of v3, /device:TPU:1, one launch (start us, length us, event | category | flops | bytes accessed | tf_op | source)
XLA Modules:
  0.0 41.5 jit_solution(17325065033285822276)
XLA Ops:
  0.0 40.7 %extend_add.1 = f32[1024,128]{1,0:T(8,128)S(1)} custom-call(f32[1024,128]{1,0:T(8,128)} %front.1, f32[1,8,1,16,256]{4,3,2,1,0:T(8,128)} %l_in.1, s32[1,8,1,512]{3,2,1,0:T(1,128)} %lmap_in.1, f32[1,8,1,16,256]{4,3,2,1,0:T(8,128)} %u_in.1, s32[1,8,1,64]{3,2,1,0:T(1,128)} %umap_in.1), custom_call_target="tpu_custom_call" | custom-call | tf_op jit(solution)/shard_map/extend_add/pallas_call | solution.py:276
  40.7 0.8 %copy.7 = f32[1024,128]{1,0:T(8,128)} copy(f32[1024,128]{1,0:T(8,128)S(1)} %extend_add.1) | data formatting | bytes 1048576

commit v4 on v3

--- a/solution.py
+++ b/solution.py
@@ -12,7 +12,7 @@
 BF16 = jnp.bfloat16
 NX, NY, NZ = 4, 4, 8
 GROUPS = ((0, 1), (2, 7), (6, 3), (4, 5))
-CHUNKS = 4
+CHUNKS = 2
 
 
 def split(value):
@@ -26,19 +26,20 @@
 
 def kernel(
     front, l_in, lmap_in, u_in, umap_in, out,
-    lbuf, ubuf, whi, wlo, hot, col_hot, packed, recv, dense, acc, mine, other, front_v, lmap, umap,
+    lbuf, ubuf, whi, wlo, hot, col_hot, packed, recv, dense, acc, other, front_v, lmap, umap,
     uy_s, uy_r, ux_s, ux_r, ly_s, z_s, z_r, res_s, res_r, ex_s, ex_r, loc,
 ):
     core, x, col = lax.axis_index("gz"), lax.axis_index("row"), lax.axis_index("col")
     y, z = lax.rem(col, NY), lax.div(col, NY)
-    peer_y = [lax.rem(y + d, NY) for d in range(NY)]
-    from_y = [lax.rem(y + NY - d, NY) for d in range(NY)]
+    turn = 1 - 2 * core
+    peer_y = [lax.rem(y + NY + turn * d, NY) for d in range(NY)]
+    from_y = [lax.rem(y + NY - turn * d, NY) for d in range(NY)]
 
     def at_y(d):
         return (core, x, z * NY + peer_y[d])
 
     def at_x(d):
-        return (core, lax.rem(x + d, NX), col)
+        return (core, lax.rem(x + NX + turn * d, NX), col)
 
     def at_z(d, dy=0):
         return (core, x, lax.rem(z + NZ + d, NZ) * NY + peer_y[dy])
@@ -203,12 +204,22 @@
         both = jnp.dot(hot[g, rows], dense[...], preferred_element_type=F32)
         return both[:, :128] + both[:, 128:]
 
+    lowest = [jnp.minimum(lax.rem(z + i, NZ), lax.rem(z + j, NZ)) * 128 for i, j in GROUPS]
+
+    def add_rows(g, chunk):
+        rows = slice(chunk * size, chunk * size + size)
+        if g == 0:
+            acc[rows] = scatter(g, chunk)
+            return
+
+        @pl.when(lowest[g] < chunk * size + size)
+        def _():
+            acc[rows] += scatter(g, chunk)
+
     def update(g):
         expand(g)
         for chunk in range(CHUNKS):
-            rows = slice(chunk * size, chunk * size + size)
-            part = scatter(g, chunk)
-            acc[rows] = part if g == 0 else acc[rows] + part
+            add_rows(g, chunk)
 
     z_start(1, (0,))
     z_start(2, (0,))
@@ -254,13 +265,13 @@
     ex = []
     for chunk in range(CHUNKS):
         rows = slice(chunk * size, chunk * size + size)
-        mine[rows] = acc[rows] + scatter(3, chunk)
-        ex.append(send(mine.at[rows], other.at[rows], ex_s.at[chunk], ex_r.at[chunk], twin))
+        add_rows(3, chunk)
+        ex.append(send(acc.at[rows], other.at[rows], ex_s.at[chunk], ex_r.at[chunk], twin))
     fetch.wait()
     for chunk in range(CHUNKS):
         rows = slice(chunk * size, chunk * size + size)
         ex[chunk].wait_recv()
-        out[rows] = front_v[rows] - (mine[rows] + other[rows])
+        out[rows] = front_v[rows] - (acc[rows] + other[rows])
     for copy in sent:
         copy.wait_send()
 
@@ -291,7 +302,6 @@
             pltpu.VMEM((1024, 128), F32),
             pltpu.VMEM((1024, 128), F32),
             pltpu.VMEM((1024, 128), F32),
-            pltpu.VMEM((1024, 128), F32),
             pltpu.VMEM((8, 1, 512), jnp.int32),
             pltpu.VMEM((8, 1, 64), jnp.int32),
             dma((3, 2)), dma((3, 2)), dma((3, 4, 2)), dma((3, 4, 2)), dma((3,)),

time: 41.6 us -> 41.1 us (0.988)
  Pallas kernels: 40.7 us -> 40.2 us
    pallas_call x1, Pallas kernels: 40.7 us -> 40.2 us  [shards(): pl.pallas_call(kernel, out_shape=jax.ShapeDtypeStruct((1024, 128), F32),...]
where the time goes in v4:
time: 41.1 us; the launch traced here: 41 us
  Pallas kernels  40.2 us (98%)
  local copies, waits for them, and re-layouts  0.8 us (2%)
    pallas_call x1, Pallas kernels, shards(): pl.pallas_call(kernel, out_shape=jax.ShapeDtypeStruct((1024, 128), F32),...  40.2 us

profile of v4, /device:TPU:1, one launch (start us, length us, event | category | flops | bytes accessed | tf_op | source)
XLA Modules:
  0.0 41.0 jit_solution(13656178207793735339)
XLA Ops:
  0.0 40.2 %extend_add.1 = f32[1024,128]{1,0:T(8,128)S(1)} custom-call(f32[1024,128]{1,0:T(8,128)} %front.1, f32[1,8,1,16,256]{4,3,2,1,0:T(8,128)} %l_in.1, s32[1,8,1,512]{3,2,1,0:T(1,128)} %lmap_in.1, f32[1,8,1,16,256]{4,3,2,1,0:T(8,128)} %u_in.1, s32[1,8,1,64]{3,2,1,0:T(1,128)} %umap_in.1), custom_call_target="tpu_custom_call" | custom-call | tf_op jit(solution)/shard_map/extend_add/pallas_call | solution.py:287
  40.2 0.8 %copy.7 = f32[1024,128]{1,0:T(8,128)} copy(f32[1024,128]{1,0:T(8,128)S(1)} %extend_add.1) | data formatting | bytes 1048576

commit v5 on v4

--- a/solution.py
+++ b/solution.py
@@ -175,7 +175,7 @@
                 bottom = prod[64:, 128 * j : 128 * j + 128]
                 packed[g, c, 2 * j] = jnp.where(lane < 64, top, pltpu.roll(bottom, 64, 1))
                 packed[g, c, 2 * j + 1] = jnp.where(lane < 64, pltpu.roll(top, 64, 1), bottom)
-            for d in (1, 3, 2):
+            for d in (2, 1, 3) if g == 3 else (1, 3, 2):
                 rc[g, c, d] = send(
                     packed.at[g, c, peer_y[d]], recv.at[g, c, d - 1],
                     res_s.at[g, c, d - 1], res_r.at[g, c, d - 1], at_y(d),

time: 41.1 us -> 41.1 us (level)
  no operation moved by 1% of the time
where the time goes in v5:
time: 41.1 us; the launch traced here: 41 us
  Pallas kernels  40.2 us (98%)
  local copies, waits for them, and re-layouts  0.8 us (2%)
    pallas_call x1, Pallas kernels, shards(): pl.pallas_call(kernel, out_shape=jax.ShapeDtypeStruct((1024, 128), F32),...  40.2 us

profile of v5, /device:TPU:1, one launch (start us, length us, event | category | flops | bytes accessed | tf_op | source)
XLA Modules:
  0.0 41.0 jit_solution(8371246577775244431)
XLA Ops:
  0.0 40.2 %extend_add.1 = f32[1024,128]{1,0:T(8,128)S(1)} custom-call(f32[1024,128]{1,0:T(8,128)} %front.1, f32[1,8,1,16,256]{4,3,2,1,0:T(8,128)} %l_in.1, s32[1,8,1,512]{3,2,1,0:T(1,128)} %lmap_in.1, f32[1,8,1,16,256]{4,3,2,1,0:T(8,128)} %u_in.1, s32[1,8,1,64]{3,2,1,0:T(1,128)} %umap_in.1), custom_call_target="tpu_custom_call" | custom-call | tf_op jit(solution)/shard_map/extend_add/pallas_call | solution.py:287
  40.2 0.8 %copy.7 = f32[1024,128]{1,0:T(8,128)} copy(f32[1024,128]{1,0:T(8,128)S(1)} %extend_add.1) | data formatting | bytes 1048576
